TPU v7x, 256 devices: a whole 4x4x8 slice. The times are simulated.
256 devices in a mesh: seq: 32 (over z, y_lo, core), chan: 8 (over y_hi, x).
Axes of the slice: x: 4, y: 4 (y_hi: 2, y_lo: 2; y = y_hi * 2 + y_lo), z: 8, core: 2. Of those that a mesh axis runs over, the one named last changes fastest.
Arguments:
- projected: bfloat16 [8192, 3, 4096], P('seq', None, 'chan'), may hold values from -6 to 6
- short_weight: float32 [3, 3, 4096], P(None, None, 'chan'), may hold values from -3 to 3
- filters: float32 [512, 8192], P(('chan', 'seq')), may hold values from -1.1 to 1.1
- skip: float32 [4096], P('chan'), may hold values from -3 to 3
- out_weight: bfloat16 [4096, 4096], P('chan', 'seq'), may hold values from -0.09375 to 0.09375
- cotangent: bfloat16 [8192, 4096], P('seq', 'chan'), may hold values from -6 to 6
Outputs:
- mixed: bfloat16 [8192, 4096], P('seq', 'chan')
- projected_grad: bfloat16 [8192, 3, 4096], P('seq', None, 'chan')
- filter_grad: float32 [512, 8192], P(('chan', 'seq'))
All inputs are finite; a program needn't handle non-finite values.
Results may differ from a plain program's by a relative error of at most 0.008.
Values may be sent and summed in bfloat16 or wider, within the bound.
No kernel may reach another device: no remote copies, remote signals or barrier semaphores. Data moves between devices by JAX's collectives and lax.ppermute only.
A program may use at most 64 MiB of HBM per device.

v0:
```python
import math
import jax
import jax.numpy as jnp
from jax import lax
from jax.sharding import PartitionSpec as P

GROUP = 8
SHORT = 3
FFT_ROWS = 128
exact_mode = lax.Precision.HIGHEST


def from_behind(shard, axis, by):
    count = lax.axis_size(axis)
    pairs = [(i, i + by) for i in range(count) if 0 <= i + by < count]
    return lax.ppermute(shard, axis, pairs)


def fourier_tables(rows_count, cols_count):
    total = rows_count * cols_count
    freq_rows = jnp.arange(rows_count, dtype=jnp.int32)
    half_rows = jnp.arange(rows_count // 2, dtype=jnp.int32)
    freq_cols = jnp.arange(cols_count, dtype=jnp.int32)
    turn = 2.0 * math.pi
    angle_first = (
        turn
        * (freq_rows[:, None] * half_rows[None, :] % rows_count).astype(jnp.float32)
        / rows_count
    )
    angle_second = (
        turn
        * (freq_cols[:, None] * freq_cols[None, :] % cols_count).astype(jnp.float32)
        / cols_count
    )
    angle_twist = (
        turn * (freq_rows[:, None] * freq_cols[None, :] % total).astype(jnp.float32) / total
    )
    return (
        jnp.cos(angle_first),
        jnp.sin(angle_first),
        jnp.cos(angle_second),
        jnp.sin(angle_second),
        jnp.cos(angle_twist),
        jnp.sin(angle_twist),
    )


def split_product(table, folded):
    table_high = table.astype(jnp.bfloat16)
    table_low = (table - table_high.astype(jnp.float32)).astype(jnp.bfloat16)
    return jnp.einsum(
        "kn,cnm->ckm", table_high, folded, preferred_element_type=jnp.float32
    ) + jnp.einsum("kn,cnm->ckm", table_low, folded, preferred_element_type=jnp.float32)


def forward_spectrum(signal, tables):
    cos_first, sin_first, cos_second, sin_second, cos_twist, sin_twist = tables
    count = signal.shape[0]
    folded = signal.reshape(count, cos_first.shape[1], cos_second.shape[0])
    if signal.dtype == jnp.bfloat16:
        first_re = split_product(cos_first, folded)
        first_im = -split_product(sin_first, folded)
    else:
        first_re = jnp.einsum("kn,cnm->ckm", cos_first, folded, precision=exact_mode)
        first_im = -jnp.einsum("kn,cnm->ckm", sin_first, folded, precision=exact_mode)
    turned_re = first_re * cos_twist + first_im * sin_twist
    turned_im = first_im * cos_twist - first_re * sin_twist
    spec_re = jnp.einsum("ckn,nm->ckm", turned_re, cos_second, precision=exact_mode) + jnp.einsum(
        "ckn,nm->ckm", turned_im, sin_second, precision=exact_mode
    )
    spec_im = jnp.einsum("ckn,nm->ckm", turned_im, cos_second, precision=exact_mode) - jnp.einsum(
        "ckn,nm->ckm", turned_re, sin_second, precision=exact_mode
    )
    return (spec_re, spec_im)


def inverse_signal(spec_re, spec_im, tables):
    cos_first, sin_first, cos_second, sin_second, cos_twist, sin_twist = tables
    count = spec_re.shape[0]
    total = cos_first.shape[0] * cos_second.shape[0]
    inner_re = jnp.einsum("ckm,mn->ckn", spec_re, cos_second, precision=exact_mode) - jnp.einsum(
        "ckm,mn->ckn", spec_im, sin_second, precision=exact_mode
    )
    inner_im = jnp.einsum("ckm,mn->ckn", spec_im, cos_second, precision=exact_mode) + jnp.einsum(
        "ckm,mn->ckn", spec_re, sin_second, precision=exact_mode
    )
    turned_re = inner_re * cos_twist - inner_im * sin_twist
    turned_im = inner_im * cos_twist + inner_re * sin_twist
    signal = jnp.einsum("kn,ckm->cnm", cos_first, turned_re, precision=exact_mode) - jnp.einsum(
        "kn,ckm->cnm", sin_first, turned_im, precision=exact_mode
    )
    return (signal / total).reshape(count, -1)


def grouped(spectrum, groups_dev):
    return spectrum.reshape(groups_dev, GROUP, spectrum.shape[1], spectrum.shape[2])


def channel_major(block):
    return lax.all_to_all(block, "seq", split_axis=0, concat_axis=1, tiled=True)


def token_major(block):
    return lax.all_to_all(block, "seq", split_axis=1, concat_axis=0, tiled=True)


def on_device(projected, short_weight, filters, skip, out_weight, cotangent):
    tok_rows = projected.shape[0]
    groups_dev = filters.shape[0]
    seq_length = filters.shape[1]
    rim = SHORT - 1
    tables = fourier_tables(FFT_ROWS, 2 * seq_length // FFT_ROWS)
    before = from_behind(projected[tok_rows - rim :], "seq", 1)
    extended = jnp.concatenate([before, projected], axis=0).astype(jnp.float32)
    short = short_weight[:, 0, :] * extended[0:tok_rows]
    for j in range(1, SHORT):
        short = short + short_weight[:, j, :] * extended[j : j + tok_rows]
    query_side = short[:, 0]
    key_side = short[:, 1]
    value_side = short[:, 2]
    carried = (key_side * value_side).astype(jnp.bfloat16)
    carried_seq = channel_major(carried.T)
    kept_re, kept_im = forward_spectrum(carried_seq, tables)
    filt_re, filt_im = forward_spectrum(filters, tables)
    group_re = grouped(kept_re, groups_dev)
    group_im = grouped(kept_im, groups_dev)
    conv_re = (group_re * filt_re[:, None] - group_im * filt_im[:, None]).reshape(kept_re.shape)
    conv_im = (group_re * filt_im[:, None] + group_im * filt_re[:, None]).reshape(kept_re.shape)
    conv_seq = inverse_signal(conv_re, conv_im, tables).astype(jnp.bfloat16)
    conv = token_major(conv_seq).T
    mixed_in = conv.astype(jnp.float32) + skip * carried.astype(jnp.float32)
    gated = (query_side * mixed_in).astype(jnp.bfloat16)
    weight_rows = lax.all_gather(out_weight, "seq", axis=1, tiled=True)
    mixed = lax.psum_scatter(
        lax.dot_general(
            weight_rows, gated, (((0,), (1,)), ((), ())), preferred_element_type=jnp.float32
        ),
        "chan",
        scatter_dimension=0,
        tiled=True,
    ).T.astype(jnp.bfloat16)
    grad_full = lax.all_gather(cotangent, "chan", axis=1, tiled=True)
    gated_grad = lax.dot_general(
        grad_full, weight_rows, (((1,), (1,)), ((), ())), preferred_element_type=jnp.float32
    )
    query_grad = gated_grad * mixed_in
    mixed_grad = (gated_grad * query_side).astype(jnp.bfloat16)
    grad_seq = channel_major(mixed_grad.T)
    grad_re, grad_im = forward_spectrum(grad_seq, tables)
    ggrad_re = grouped(grad_re, groups_dev)
    ggrad_im = grouped(grad_im, groups_dev)
    back_re = (ggrad_re * filt_re[:, None] + ggrad_im * filt_im[:, None]).reshape(grad_re.shape)
    back_im = (ggrad_im * filt_re[:, None] - ggrad_re * filt_im[:, None]).reshape(grad_re.shape)
    back_seq = inverse_signal(back_re, back_im, tables).astype(jnp.bfloat16)
    back = token_major(back_seq).T
    cross_re = jnp.sum(ggrad_re * group_re + ggrad_im * group_im, axis=1)
    cross_im = jnp.sum(ggrad_im * group_re - ggrad_re * group_im, axis=1)
    filter_grad = inverse_signal(cross_re, cross_im, tables) * (1.0 / math.sqrt(GROUP * seq_length))
    carried_grad = back.astype(jnp.float32) + skip * mixed_grad.astype(jnp.float32)
    short_grad = jnp.stack([query_grad, carried_grad * value_side, carried_grad * key_side], axis=1)
    after = from_behind(short_grad[:rim], "seq", -1)
    extended_grad = jnp.concatenate([short_grad, after], axis=0)
    projected_grad = short_weight[:, 0, :] * extended_grad[rim : rim + tok_rows]
    for j in range(1, SHORT):
        projected_grad = (
            projected_grad + short_weight[:, j, :] * extended_grad[rim - j : rim - j + tok_rows]
        )
    return (mixed, projected_grad.astype(jnp.bfloat16), filter_grad)


def solution(mesh):
    placed = (
        P("seq", None, "chan"),
        P(None, None, "chan"),
        P(("chan", "seq"), None),
        P("chan"),
        P("chan", "seq"),
        P("seq", "chan"),
    )
    return jax.shard_map(
        on_device,
        mesh=mesh,
        in_specs=placed,
        out_specs=(P("seq", "chan"), P("seq", None, "chan"), P(("chan", "seq"), None)),
        check_vma=False,
    )
```

profile of v0, /device:TPU:2, one launch (start us, length us, event | category | flops | bytes accessed | tf_op | source)
XLA Modules:
  0.0 367.4 jit_solution(16333220502571178986)
XLA Ops:
  8.0 0.7 all-gather.3.cloned.1.call-update
  8.7 0.7 slice.43
  9.4 1.7 collective-permute-start
  11.5 0.9 fusion.347
  12.3 1.3 convolution_negate_fusion
  13.6 1.3 fusion.68
  16.2 59.0 %all-gather.5.cloned.1.call-done = bf16[256,4096]{1,0:T(8,128)(2,1)} async-done(((bf16[256,512]{1,0:T(8,128)(2,1)}), bf16[256,4096]{1,0:T(8,128)(2,1)}) %all-gather.5.cloned.1.call-update) | async-done | bytes 2097168 | tf_op jit(solution)/shard_map/all_gather | solution.py:142
  75.2 73.1 %all-gather.3.cloned.1.call-done = bf16[512,4096]{1,0:T(8,128)(2,1)} async-done(((bf16[512,128]{1,0:T(8,128)(2,1)}), bf16[512,4096]{1,0:T(8,128)(2,1)}) %all-gather.3.cloned.1.call-update) | async-done | bytes 4194320 | tf_op jit(solution)/shard_map/all_gather | solution.py:133
  148.3 4.9 %multiply_convert_fusion = (bf16[256,512]{1,0:T(8,128)(2,1)S(1)}, f32[256,512]{1,0:T(8,128)}) fusion(f32[256,3,512]{2,0,1:T(8,128)S(1)} %fusion.3, bf16[256,4096]{1,0:T(8,128)(2,1)} %all-gather.5.cloned.1.call-done, bf16[512,4096]{1,0:T(8,128)(2,1)} %all-gather.3.cloned.1.call-done), kind=kOutput, calls=%fused_computation.89 | convolution fusion | flops 1074003968 | bytes 7602176 | tf_op jit(solution)/shard_map/dot_general | solution.py:143
  153.2 0.8 copy.51
  154.0 5.3 %all-to-all-start.2 = ((bf16[32,16,256]{2,1,0:T(8,128)(2,1)}), bf16[32,16,256]{2,1,0:T(8,128)(2,1)S(1)}, u32[]{:S(2)}, u32[]{:S(2)}) async-start(bf16[32,16,256]{2,1,0:T(8,128)(2,1)} %bitcast.28), calls=%async_computation.3 | async-start | bytes 524288 | tf_op jit(solution)/shard_map/all_to_all | solution.py:100
  161.3 10.3 %all-to-all-done.2 = bf16[32,16,256]{2,1,0:T(8,128)(2,1)S(1)} async-done(((bf16[32,16,256]{2,1,0:T(8,128)(2,1)}), bf16[32,16,256]{2,1,0:T(8,128)(2,1)S(1)}, u32[]{:S(2)}, u32[]{:S(2)}) %all-to-all-start.2) | async-done | bytes 262176 | tf_op jit(solution)/shard_map/all_to_all | solution.py:100
  173.6 2.1 fusion.48
  175.6 2.1 fusion.47
  177.7 2.1 convolution_subtract_fusion.1
  179.8 3.1 fusion.21
  182.9 1.6 fusion.88
  184.5 1.3 fusion.86
  185.8 1.4 convolution_subtract_fusion
  187.2 1.3 convolution_add_fusion
  188.6 1.5 fusion.26
  190.1 1.5 fusion.15
  191.8 15.3 %all_to_all.52 = bf16[16,32,256]{2,0,1:T(8,128)(2,1)S(1)} all-to-all(bf16[16,32,256]{2,0,1:T(8,128)(2,1)S(1)} %copy.63), channel_id=1, replica_groups=mesh['seq'=32,'chan'=8] {'seq'}, dimensions={1} | all-to-all | bytes 524288 | tf_op jit(solution)/shard_map/all_to_all | solution.py:104
  207.5 1.4 multiply_bitcast_fusion.1
  209.0 15.4 %all_to_all.53 = bf16[32,16,256]{2,1,0:T(8,128)(2,1)S(1)} all-to-all(bf16[32,16,256]{2,1,0:T(8,128)(2,1)S(1)} %bitcast.243), channel_id=1, replica_groups=mesh['seq'=32,'chan'=8] {'seq'}, dimensions={0} | all-to-all | bytes 524288 | tf_op jit(solution)/shard_map/all_to_all | solution.py:100
  226.3 2.1 fusion.46
  228.4 2.1 fusion.45
  230.5 2.1 convolution_subtract_fusion.3
  232.6 3.1 fusion.19
  235.7 1.3 fusion.94
  237.0 1.5 fusion.92
  238.6 1.4 convolution_subtract_fusion.2
  239.9 1.3 convolution_add_fusion.2
  241.3 1.5 fusion.33
  242.8 2.2 fusion.16
  245.0 1.7 convert_element_type.266
  246.7 1.1 copy.49
  247.8 15.4 %all_to_all.54 = bf16[16,32,256]{2,0,1:T(8,128)(2,1)S(1)} all-to-all(bf16[16,32,256]{2,0,1:T(8,128)(2,1)S(1)} %copy.49), channel_id=1, replica_groups=mesh['seq'=32,'chan'=8] {'seq'}, dimensions={1} | all-to-all | bytes 524288 | tf_op jit(solution)/shard_map/all_to_all | solution.py:104
  263.2 0.9 convert_element_type.289
  264.1 2.1 copy.50
  266.1 5.8 %convolution_bitcast_fusion = f32[4096,256]{0,1:T(8,128)} fusion(bf16[512,4096]{1,0:T(8,128)(2,1)} %all-gather.3.cloned.1.call-done, f32[256,3,512]{2,0,1:T(8,128)} %copy-done, bf16[256,512]{1,0:T(8,128)(2,1)S(1)} %get-tuple-element.11, f32[512,256]{0,1:T(8,128)} %copy.50, f32[512]{0:T(512)S(1)} %copy-done.15), kind=kOutput, calls=%fused_computation | convolution fusion | flops 1074397184 | bytes 9701376 | tf_op jit(solution)/shard_map/dot_general | solution.py:135
  272.0 2.1 bitcast_reduce_fusion.1
  276.8 1.3 collective-permute-start.1
  278.5 0.7 copy.102
  279.2 0.7 collective-permute-done.1
  280.1 1.4 fusion.2
  281.5 77.4 %reduce-scatter.2.cloned.1.call-done = f32[512,256]{0,1:T(8,128)} async-done(((f32[4096,256]{0,1:T(8,128)}), f32[512,256]{0,1:T(8,128)}) %reduce-scatter.2.cloned.1.call-update) | async-done | bytes 524304 | tf_op jit(solution)/shard_map/reduce_scatter | solution.py:134
  358.9 1.8 convert_bitcast_fusion
  (78 shorter events, 11.8 us)
Async XLA Ops:
  7.2 8.3 %copy-start.10 = (bf16[256,3,512]{2,0,1:T(8,128)(2,1)S(1)}, bf16[256,3,512]{2,0,1:T(8,128)(2,1)}, u32[]{:S(2)}) copy-start(bf16[256,3,512]{2,0,1:T(8,128)(2,1)} %param.6) | copy-start | bytes 2359300
  7.2 68.0 %all-gather.5.cloned.1.call-start = ((), (), s32[]{:S(2)}) async-start(), calls=%async_computation.7 | async-start | bytes 2359296 | tf_op jit(solution)/shard_map/all_gather | solution.py:142
  7.9 140.4 %all-gather.3.cloned.1.call-start = ((), (), s32[]{:S(2)}) async-start(), calls=%async_computation.5 | async-start | bytes 4325376 | tf_op jit(solution)/shard_map/all_gather | solution.py:133
  9.4 6.1 %collective-permute-start = (bf16[2,3,512]{2,0,1:T(2,128)(2,1)S(1)}, bf16[2,3,512]{2,0,1:T(2,128)(2,1)S(1)}, u32[]{:S(2)}, u32[]{:S(2)}) collective-permute-start(bf16[2,3,512]{2,0,1:T(2,128)(2,1)S(1)} %slice.43), channel_id=1, source_target_pairs={{0,8},{8,16},{16,24},{24,32},{32,40},{40,48},{48,56},{56,64},{64,7... | collective-permute-start | bytes 18440 | tf_op jit(solution)/shard_map/ppermute | solution.py:16
  11.4 149.3 %copy-start.2 = (f32[128,128]{1,0:T(8,128)}, f32[128,128]{1,0:T(8,128)S(1)}, u32[]{:S(2)}) copy-start(f32[128,128]{1,0:T(8,128)S(1)} %get-tuple-element.21) | copy-start | bytes 196612
  11.4 149.3 %copy-start.4 = (f32[128,128]{1,0:T(8,128)}, f32[128,128]{1,0:T(8,128)S(1)}, u32[]{:S(2)}) copy-start(f32[128,128]{1,0:T(8,128)S(1)} %get-tuple-element.22) | copy-start | bytes 196612
  15.5 0.7 copy-start.12
  16.2 137.0 %copy-start = (f32[256,3,512]{2,0,1:T(8,128)}, f32[256,3,512]{2,0,1:T(8,128)S(1)}, u32[]{:S(2)}) copy-start(f32[256,3,512]{2,0,1:T(8,128)S(1)} %fusion.3) | copy-start | bytes 4718596
  154.0 17.7 %all-to-all-start.2 = ((bf16[32,16,256]{2,1,0:T(8,128)(2,1)}), bf16[32,16,256]{2,1,0:T(8,128)(2,1)S(1)}, u32[]{:S(2)}, u32[]{:S(2)}) async-start(bf16[32,16,256]{2,1,0:T(8,128)(2,1)} %bitcast.28), calls=%async_computation.3 | async-start | bytes 524288 | tf_op jit(solution)/shard_map/all_to_all | solution.py:100
  159.3 199.6 %reduce-scatter.2.cloned.1.call-start = ((), (), s32[]{:S(2)}) async-start(), calls=%async_computation.6 | async-start | bytes 4718592 | tf_op jit(solution)/shard_map/reduce_scatter | solution.py:134
  160.8 19.0 %copy-start.6 = (f32[2,128,128]{2,1,0:T(8,128)}, f32[2,128,128]{2,1,0:T(8,128)S(1)}, u32[]{:S(2)}) copy-start(f32[2,128,128]{2,1,0:T(8,128)S(1)} %convolution_subtract_fusion.7) | copy-start | bytes 393220
  161.3 18.5 %copy-start.8 = (f32[2,128,128]{2,1,0:T(8,128)}, f32[2,128,128]{2,1,0:T(8,128)S(1)}, u32[]{:S(2)}) copy-start(f32[2,128,128]{2,1,0:T(8,128)S(1)} %convolution_add_fusion.9) | copy-start | bytes 393220
  191.7 15.8 %copy-start.14 = (f32[512]{0:T(512)S(1)}, f32[512]{0:T(512)}, u32[]{:S(2)}) copy-start(f32[512]{0:T(512)} %param.9) | copy-start | bytes 6148
  230.4 2.1 copy-start.7
  230.4 2.1 copy-start.9
  246.7 19.4 %copy-start.15 = (f32[512]{0:T(512)S(1)}, f32[512]{0:T(512)}, u32[]{:S(2)}) copy-start(f32[512]{0:T(512)} %param.9) | copy-start | bytes 6148
  272.0 4.2 %copy-start.3 = (f32[128,128]{1,0:T(8,128)S(1)}, f32[128,128]{1,0:T(8,128)}, u32[]{:S(2)}) copy-start(f32[128,128]{1,0:T(8,128)} %copy-done.2) | copy-start | bytes 196612
  272.0 4.2 %copy-start.5 = (f32[128,128]{1,0:T(8,128)S(1)}, f32[128,128]{1,0:T(8,128)}, u32[]{:S(2)}) copy-start(f32[128,128]{1,0:T(8,128)} %copy-done.4) | copy-start | bytes 196612
  274.1 2.5 copy-start.1
  274.1 2.5 copy-start.11
  274.1 2.5 copy-start.16
  276.8 3.1 collective-permute-start.1
  279.2 0.9 copy-start.13
Sparse Core Ops, SparseCore 0:
  10.5 64.6 all-gather.4
  76.9 71.2 all-gather.2
  272.1 86.7 reduce-scatter.1
where the time goes:
time: 372 us; the launch traced here: 367 us
  waiting for transfers between devices  222 us (60%)
  matrix products  58 us (16%)
  blocking collectives  46.1 us (12%)
  between operations  14.6 us (4%)
  local copies, waits for them, and re-layouts  9.25 us (2%)
  other arithmetic  8.93 us (2%)
  starting transfers between devices  8.58 us (2%)
    reduce_scatter x1, waiting for transfers between devices, on_device(): lax.psum_scatter(lax.dot_general(weight_rows, gated, (((0,), (1,)), ((),...  77.4 us
    all_gather x1, waiting for transfers between devices, on_device(): weight_rows = lax.all_gather(out_weight, 'seq', axis=1, tiled=True)  73.1 us
    all_gather x1, waiting for transfers between devices, on_device(): grad_full = lax.all_gather(cotangent, 'chan', axis=1, tiled=True)  59 us
    all_to_all x2, blocking collectives, token_major(): return lax.all_to_all(block, 'seq', split_axis=1, concat_axis=0, tiled=True)  30.7 us
    all_to_all x1, blocking collectives, channel_major(): return lax.all_to_all(block, 'seq', split_axis=0, concat_axis=1, tiled=True)  15.4 us
    all_to_all x1, waiting for transfers between devices, channel_major(): return lax.all_to_all(block, 'seq', split_axis=0, concat_axis=1, tiled=True)  10.3 us
  transfers between devices with their start and end apart: 6, of which 5 were waited for; matrix products, arithmetic and copies ran while one was open for 4% of the time, Pallas kernels for 0%

commit v1 on v0

--- a/solution.py
+++ b/solution.py
@@ -139,7 +139,10 @@
         scatter_dimension=0,
         tiled=True,
     ).T.astype(jnp.bfloat16)
-    grad_full = lax.all_gather(cotangent, "chan", axis=1, tiled=True)
+    size = lax.axis_size("chan")
+    blocks = jnp.stack([cotangent for _ in range(size)])
+    blocks = lax.all_to_all(blocks, "chan", split_axis=0, concat_axis=0)
+    grad_full = jnp.concatenate(blocks, axis=1)
     gated_grad = lax.dot_general(
         grad_full, weight_rows, (((1,), (1,)), ((), ())), preferred_element_type=jnp.float32
     )

time: 372 us -> 325 us (0.87)
  waiting for transfers between devices: 222 us -> 168 us
  starting transfers between devices: 8.58 us -> 15.8 us
    all_gather x1 -> x0, waiting for transfers between devices: 59 us -> none  [on_device(): grad_full = lax.all_gather(cotangent, 'chan', axis=1, tiled=True)]
    all_to_all x0 -> x1, waiting for transfers between devices: none -> 23.5 us  [on_device(): blocks = lax.all_to_all(blocks, 'chan', split_axis=0, concat_axis=0)]
    all_gather x1, waiting for transfers between devices: 73.1 us -> 55.2 us  [on_device(): weight_rows = lax.all_gather(out_weight, 'seq', axis=1, tiled=True)]
    all_to_all x0 -> x1, starting transfers between devices: none -> 7.59 us  [on_device(): blocks = lax.all_to_all(blocks, 'chan', split_axis=0, concat_axis=0)]
where the time goes in v1:
time: 325 us; the launch traced here: 320 us
  waiting for transfers between devices  168 us (52%)
  matrix products  56.3 us (17%)
  blocking collectives  46.1 us (14%)
  starting transfers between devices  15.8 us (5%)
  between operations  14.9 us (5%)
  local copies, waits for them, and re-layouts  10.3 us (3%)
  other arithmetic  8.94 us (3%)
    reduce_scatter x1, waiting for transfers between devices, on_device(): lax.psum_scatter(lax.dot_general(weight_rows, gated, (((0,), (1,)), ((),...  77.3 us
    all_gather x1, waiting for transfers between devices, on_device(): weight_rows = lax.all_gather(out_weight, 'seq', axis=1, tiled=True)  55.2 us
    all_to_all x2, blocking collectives, token_major(): return lax.all_to_all(block, 'seq', split_axis=1, concat_axis=0, tiled=True)  30.7 us
    all_to_all x1, waiting for transfers between devices, on_device(): blocks = lax.all_to_all(blocks, 'chan', split_axis=0, concat_axis=0)  23.5 us
    all_to_all x1, blocking collectives, channel_major(): return lax.all_to_all(block, 'seq', split_axis=0, concat_axis=1, tiled=True)  15.4 us
    all_to_all x1, waiting for transfers between devices, channel_major(): return lax.all_to_all(block, 'seq', split_axis=0, concat_axis=1, tiled=True)  10.4 us
    all_to_all x1, starting transfers between devices, on_device(): blocks = lax.all_to_all(blocks, 'chan', split_axis=0, concat_axis=0)  7.59 us
    dot_general x3, matrix products, forward_spectrum(): jnp.einsum('ckn,nm->ckm', turned_im, sin_second, precision=exact_mode)  6.78 us
  transfers between devices with their start and end apart: 6, of which 5 were waited for; matrix products, arithmetic and copies ran while one was open for 4% of the time, Pallas kernels for 0%

profile of v1, /device:TPU:2, one launch (start us, length us, event | category | flops | bytes accessed | tf_op | source)
XLA Modules:
  0.0 320.2 jit_solution(9123159588376874152)
XLA Ops:
  7.2 0.7 all-gather.2.cloned.1.call-update
  7.9 1.1 copy.51
  9.0 1.5 stack.10
  10.5 7.6 %all-to-all-start.2 = ((bf16[8,256,512]{1,2,0:T(8,128)(2,1)}), bf16[8,256,512]{1,2,0:T(8,128)(2,1)}, u32[]{:S(2)}, u32[]{:S(2)}) async-start(bf16[8,256,512]{1,2,0:T(8,128)(2,1)} %stack.10), calls=%async_computation.3 | async-start | bytes 4194304 | tf_op jit(solution)/shard_map/all_to_all | solution.py:144
  18.1 1.3 collective-permute-start
  20.7 0.5 fusion.50
  22.0 23.5 %all-to-all-done.2 = bf16[8,256,512]{1,2,0:T(8,128)(2,1)} async-done(((bf16[8,256,512]{1,2,0:T(8,128)(2,1)}), bf16[8,256,512]{1,2,0:T(8,128)(2,1)}, u32[]{:S(2)}, u32[]{:S(2)}) %all-to-all-start.2) | async-done | bytes 2097184 | tf_op jit(solution)/shard_map/all_to_all | solution.py:144
  45.5 55.2 %all-gather.2.cloned.1.call-done = bf16[512,4096]{1,0:T(8,128)(2,1)} async-done(((bf16[512,128]{1,0:T(8,128)(2,1)}), bf16[512,4096]{1,0:T(8,128)(2,1)}) %all-gather.2.cloned.1.call-update) | async-done | bytes 4194320 | tf_op jit(solution)/shard_map/all_gather | solution.py:133
  100.7 4.9 %multiply_convert_fusion = (bf16[256,512]{1,0:T(8,128)(2,1)S(1)}, f32[256,512]{1,0:T(8,128)}) fusion(f32[256,3,512]{2,0,1:T(8,128)S(1)} %fusion.3, bf16[256,4096]{0,1:T(8,128)(2,1)} %bitcast.27, bf16[512,4096]{1,0:T(8,128)(2,1)} %all-gather.2.cloned.1.call-done), kind=kOutput, calls=%fused_computation.89 | convolution fusion | flops 1074003968 | bytes 7602176 | tf_op jit(solution)/shard_map/dot_general | solution.py:146
  105.6 0.8 copy.52
  106.5 5.4 %all-to-all-start.3 = ((bf16[32,16,256]{2,1,0:T(8,128)(2,1)}), bf16[32,16,256]{2,1,0:T(8,128)(2,1)S(1)}, u32[]{:S(2)}, u32[]{:S(2)}) async-start(bf16[32,16,256]{2,1,0:T(8,128)(2,1)} %bitcast.30), calls=%async_computation.4 | async-start | bytes 524288 | tf_op jit(solution)/shard_map/all_to_all | solution.py:100
  113.9 10.4 %all-to-all-done.3 = bf16[32,16,256]{2,1,0:T(8,128)(2,1)S(1)} async-done(((bf16[32,16,256]{2,1,0:T(8,128)(2,1)}), bf16[32,16,256]{2,1,0:T(8,128)(2,1)S(1)}, u32[]{:S(2)}, u32[]{:S(2)}) %all-to-all-start.3) | async-done | bytes 262176 | tf_op jit(solution)/shard_map/all_to_all | solution.py:100
  126.1 2.1 fusion.48
  128.2 2.1 fusion.47
  130.3 2.1 convolution_subtract_fusion.1
  132.4 3.1 fusion.21
  135.5 1.6 fusion.88
  137.1 1.3 fusion.86
  138.4 1.4 convolution_subtract_fusion
  139.8 1.3 convolution_add_fusion
  141.1 1.5 fusion.26
  142.6 1.5 fusion.15
  144.4 15.3 %all_to_all.57 = bf16[16,32,256]{2,0,1:T(8,128)(2,1)S(1)} all-to-all(bf16[16,32,256]{2,0,1:T(8,128)(2,1)S(1)} %copy.64), channel_id=1, replica_groups=mesh['seq'=32,'chan'=8] {'seq'}, dimensions={1} | all-to-all | bytes 524288 | tf_op jit(solution)/shard_map/all_to_all | solution.py:104
  160.0 1.4 multiply_bitcast_fusion.1
  161.6 15.4 %all_to_all.58 = bf16[32,16,256]{2,1,0:T(8,128)(2,1)S(1)} all-to-all(bf16[32,16,256]{2,1,0:T(8,128)(2,1)S(1)} %bitcast.246), channel_id=1, replica_groups=mesh['seq'=32,'chan'=8] {'seq'}, dimensions={0} | all-to-all | bytes 524288 | tf_op jit(solution)/shard_map/all_to_all | solution.py:100
  178.9 2.1 fusion.46
  180.9 2.1 fusion.45
  183.0 2.1 convolution_subtract_fusion.3
  185.1 3.1 fusion.19
  188.2 1.3 fusion.94
  189.6 1.5 fusion.92
  191.1 1.4 convolution_subtract_fusion.2
  192.5 1.3 convolution_add_fusion.2
  193.8 1.5 fusion.33
  195.3 2.2 fusion.16
  197.6 1.8 convert_element_type.266
  199.3 1.1 copy.49
  200.4 15.4 %all_to_all.59 = bf16[16,32,256]{2,0,1:T(8,128)(2,1)S(1)} all-to-all(bf16[16,32,256]{2,0,1:T(8,128)(2,1)S(1)} %copy.49), channel_id=1, replica_groups=mesh['seq'=32,'chan'=8] {'seq'}, dimensions={1} | all-to-all | bytes 524288 | tf_op jit(solution)/shard_map/all_to_all | solution.py:104
  215.8 0.9 convert_element_type.289
  216.7 2.1 copy.50
  218.7 5.8 %convolution_bitcast_fusion = f32[4096,256]{0,1:T(8,128)} fusion(bf16[512,4096]{1,0:T(8,128)(2,1)} %all-gather.2.cloned.1.call-done, f32[256,3,512]{2,0,1:T(8,128)} %copy-done, bf16[256,512]{1,0:T(8,128)(2,1)S(1)} %get-tuple-element.11, f32[512,256]{0,1:T(8,128)} %copy.50, f32[512]{0:T(512)S(1)} %copy-done.16), kind=kOutput, calls=%fused_computation | convolution fusion | flops 1074397184 | bytes 9701376 | tf_op jit(solution)/shard_map/dot_general | solution.py:135
  224.6 2.1 bitcast_reduce_fusion.1
  229.4 1.3 collective-permute-start.1
  231.1 0.7 copy.103
  231.8 0.7 collective-permute-done.1
  232.7 1.4 fusion.2
  234.1 77.3 %reduce-scatter.2.cloned.1.call-done = f32[512,256]{0,1:T(8,128)} async-done(((f32[4096,256]{0,1:T(8,128)}), f32[512,256]{0,1:T(8,128)}) %reduce-scatter.2.cloned.1.call-update) | async-done | bytes 524304 | tf_op jit(solution)/shard_map/reduce_scatter | solution.py:134
  311.4 1.8 convert_bitcast_fusion
  (83 shorter events, 11.5 us)
Async XLA Ops:
  7.2 93.5 %all-gather.2.cloned.1.call-start = ((), (), s32[]{:S(2)}) async-start(), calls=%async_computation.6 | async-start | bytes 4325376 | tf_op jit(solution)/shard_map/all_gather | solution.py:133
  10.5 7.6 %copy-start.10 = (bf16[256,3,512]{2,0,1:T(8,128)(2,1)S(1)}, bf16[256,3,512]{2,0,1:T(8,128)(2,1)}, u32[]{:S(2)}) copy-start(bf16[256,3,512]{2,0,1:T(8,128)(2,1)} %param.6) | copy-start | bytes 2359300
  10.5 9.2 %copy-start.18 = (f32[3,3,512]{2,1,0:T(4,128)S(1)}, f32[3,3,512]{2,1,0:T(4,128)}, u32[]{:S(2)}) copy-start(f32[3,3,512]{2,1,0:T(4,128)} %param.7) | copy-start | bytes 55300
  10.5 9.2 %copy-start.12 = (f32[2,8192]{1,0:T(2,128)S(1)}, f32[2,8192]{1,0:T(2,128)}, u32[]{:S(2)}) copy-start(f32[2,8192]{1,0:T(2,128)} %param.8) | copy-start | bytes 196612
  10.5 35.0 %all-to-all-start.2 = ((bf16[8,256,512]{1,2,0:T(8,128)(2,1)}), bf16[8,256,512]{1,2,0:T(8,128)(2,1)}, u32[]{:S(2)}, u32[]{:S(2)}) async-start(bf16[8,256,512]{1,2,0:T(8,128)(2,1)} %stack.10), calls=%async_computation.3 | async-start | bytes 4194304 | tf_op jit(solution)/shard_map/all_to_all | solution.py:144
  18.1 3.1 collective-permute-start
  19.7 93.6 %copy-start.2 = (f32[128,128]{1,0:T(8,128)}, f32[128,128]{1,0:T(8,128)S(1)}, u32[]{:S(2)}) copy-start(f32[128,128]{1,0:T(8,128)S(1)} %get-tuple-element.21) | copy-start | bytes 196612
  19.7 93.6 %copy-start.4 = (f32[128,128]{1,0:T(8,128)}, f32[128,128]{1,0:T(8,128)S(1)}, u32[]{:S(2)}) copy-start(f32[128,128]{1,0:T(8,128)S(1)} %get-tuple-element.22) | copy-start | bytes 196612
  21.2 0.7 copy-start.13
  22.0 83.6 %copy-start = (f32[256,3,512]{2,0,1:T(8,128)}, f32[256,3,512]{2,0,1:T(8,128)S(1)}, u32[]{:S(2)}) copy-start(f32[256,3,512]{2,0,1:T(8,128)S(1)} %fusion.3) | copy-start | bytes 4718596
  106.5 17.8 %all-to-all-start.3 = ((bf16[32,16,256]{2,1,0:T(8,128)(2,1)}), bf16[32,16,256]{2,1,0:T(8,128)(2,1)S(1)}, u32[]{:S(2)}, u32[]{:S(2)}) async-start(bf16[32,16,256]{2,1,0:T(8,128)(2,1)} %bitcast.30), calls=%async_computation.4 | async-start | bytes 524288 | tf_op jit(solution)/shard_map/all_to_all | solution.py:100
  111.8 199.5 %reduce-scatter.2.cloned.1.call-start = ((), (), s32[]{:S(2)}) async-start(), calls=%async_computation.7 | async-start | bytes 4718592 | tf_op jit(solution)/shard_map/reduce_scatter | solution.py:134
  113.3 19.0 %copy-start.6 = (f32[2,128,128]{2,1,0:T(8,128)}, f32[2,128,128]{2,1,0:T(8,128)S(1)}, u32[]{:S(2)}) copy-start(f32[2,128,128]{2,1,0:T(8,128)S(1)} %convolution_subtract_fusion.7) | copy-start | bytes 393220
  113.8 18.5 %copy-start.8 = (f32[2,128,128]{2,1,0:T(8,128)}, f32[2,128,128]{2,1,0:T(8,128)S(1)}, u32[]{:S(2)}) copy-start(f32[2,128,128]{2,1,0:T(8,128)S(1)} %convolution_add_fusion.9) | copy-start | bytes 393220
  144.2 15.8 %copy-start.15 = (f32[512]{0:T(512)S(1)}, f32[512]{0:T(512)}, u32[]{:S(2)}) copy-start(f32[512]{0:T(512)} %param.9) | copy-start | bytes 6148
  183.0 2.1 copy-start.7
  183.0 2.1 copy-start.9
  199.3 19.4 %copy-start.16 = (f32[512]{0:T(512)S(1)}, f32[512]{0:T(512)}, u32[]{:S(2)}) copy-start(f32[512]{0:T(512)} %param.9) | copy-start | bytes 6148
  224.6 4.2 %copy-start.3 = (f32[128,128]{1,0:T(8,128)S(1)}, f32[128,128]{1,0:T(8,128)}, u32[]{:S(2)}) copy-start(f32[128,128]{1,0:T(8,128)} %copy-done.2) | copy-start | bytes 196612
  224.6 4.2 %copy-start.5 = (f32[128,128]{1,0:T(8,128)S(1)}, f32[128,128]{1,0:T(8,128)}, u32[]{:S(2)}) copy-start(f32[128,128]{1,0:T(8,128)} %copy-done.4) | copy-start | bytes 196612
  226.6 2.5 copy-start.1
  226.6 2.5 copy-start.11
  226.7 2.5 copy-start.17
  229.4 3.1 collective-permute-start.1
  231.8 0.9 copy-start.14
Sparse Core Ops, SparseCore 0:
  9.7 90.9 all-gather.1
  224.7 86.6 reduce-scatter.1
